TPU v7x, 32 devices: a whole 2x2x4 slice. The times are simulated.
32 devices in a mesh: section: 2 (over x), dp: 16 (over z, y, core).
Axes of the slice: x: 2, y: 2, z: 4, core: 2. Of those that a mesh axis runs over, the one named last changes fastest.
Arguments:
- edge_data: bfloat16 [2, 2, 1024, 960], P('section', None, 'dp'), may hold values from -6 to 6
- segment_ids: int32 [2, 1024], P(None, 'dp'), may hold values from 0 to 63, as said below
- attn_weight: bfloat16 [2, 960, 2560], P('section', None, 'dp'), may hold values from -0.1875 to 0.1875
- ffn_weight: bfloat16 [2, 3, 960, 2560], P('section', None, None, 'dp'), may hold values from -0.1875 to 0.1875
- gains: bfloat16 [2, 1920], P('section', 'dp'), may hold values from 0.5 to 1.5
Outputs:
- edge_out: bfloat16 [2, 2, 1024, 960], P('section', None, 'dp')
- attention_grad: float32 [2, 960, 2560], P('section', None, 'dp')
- ffn_grad: float32 [2, 3, 960, 2560], P('section', None, None, 'dp')
- gain_grad: float32 [2, 1920], P('section', 'dp')
Inputs may be any that keep to these rules, and one draw needn't show every extreme that they name: `segment_ids`: inside each aligned block of 64 tokens (one index of dp in one micro-batch) the ids start at 0 at the block's first token and rise by 0 or 1 from token to token; tokens of a block with equal ids form one sequence; no sequence crosses a block; some sequence fills a whole block, and some block holds only sequences of one token.
All inputs are finite; a program needn't handle non-finite values.
Results may differ from a plain program's by a relative error of at most 0.02.
Values may be sent and summed in bfloat16 or wider, within the bound.
No kernel may reach another device: no remote copies, remote signals or barrier semaphores. Data moves between devices by JAX's collectives and lax.ppermute only.
A program may use at most 256 MiB of HBM per device.

v0:
```python
import jax
import jax.numpy as jnp
from jax import lax
from jax.sharding import PartitionSpec as P

QUERY_HEADS = 15
KEY_VALUE_HEADS = 5
HEAD_SIZE = 64


epsilon = 1e-05
theta_base = 100000.0
contract_last = (((1,), (1,)), ((), ()))
contract_first = (((0,), (0,)), ((), ()))


def passed_along(array, axis, by):
    length = lax.axis_size(axis)
    pairs = [(i, i + by) for i in range(length) if 0 <= i + by < length]
    return lax.ppermute(array, axis, pairs)


def matmul(left_op, right_op):
    return jnp.dot(left_op, right_op, preferred_element_type=jnp.float32)


def right_trans(left_op, right_op):
    return lax.dot_general(left_op, right_op, contract_last, preferred_element_type=jnp.float32)


def left_trans(left_op, right_op):
    return lax.dot_general(left_op, right_op, contract_first, preferred_element_type=jnp.float32)


def norm_rows(rows, gain):
    return rows * lax.rsqrt(jnp.mean(rows * rows, axis=-1, keepdims=True) + epsilon) * gain


def rotary_apply(rows, cosine_table, sine_values):
    half_size = rows.shape[-1] // 2
    front_part = rows[..., :half_size]
    back_part = rows[..., half_size:]
    return jnp.concatenate(
        [
            front_part * cosine_table - back_part * sine_values,
            back_part * cosine_table + front_part * sine_values,
        ],
        axis=-1,
    )


def block_tables(segments):
    block_len = segments.shape[-1]
    offsets = jnp.arange(block_len, dtype=jnp.int32)
    same_segment = segments[..., :, None] == segments[..., None, :]
    segment_start = jnp.min(jnp.where(same_segment, offsets, block_len), axis=-1)
    positions = (offsets - segment_start).astype(jnp.float32)
    half_size = HEAD_SIZE // 2
    frequency = theta_base ** (-(2.0 * jnp.arange(half_size, dtype=jnp.float32)) / HEAD_SIZE)
    angles = positions[..., None] * frequency
    allowed = same_segment & (offsets[:, None] >= offsets[None, :])
    return (jnp.cos(angles), jnp.sin(angles), allowed)


def attention_scores(query_matrix, key_matrix_rows, allowed):
    scores = jnp.einsum(
        "tgrd,ugd->grtu", query_matrix, key_matrix_rows, preferred_element_type=jnp.float32
    ) * HEAD_SIZE ** (-0.5)
    return jnp.where(allowed, scores, -1000000000.0)


def layer_forward(layer_in, qkv_w, out_w, ffn_w, gain_row, cosine_table, sine_values, allowed):
    sequence_length, model_width = layer_in.shape
    head_column_width = QUERY_HEADS * HEAD_SIZE
    key_value_width = KEY_VALUE_HEADS * HEAD_SIZE
    query_group_count = QUERY_HEADS // KEY_VALUE_HEADS
    residual = layer_in.astype(jnp.float32)
    normed = norm_rows(residual, gain_row[:model_width].astype(jnp.float32)).astype(jnp.bfloat16)
    projected_rows = matmul(normed, qkv_w)
    query_matrix = rotary_apply(
        projected_rows[:, :head_column_width].reshape(
            sequence_length, KEY_VALUE_HEADS, query_group_count, HEAD_SIZE
        ),
        cosine_table[:, None, None, :],
        sine_values[:, None, None, :],
    ).astype(jnp.bfloat16)
    key_matrix_rows = rotary_apply(
        projected_rows[:, head_column_width : head_column_width + key_value_width].reshape(
            sequence_length, KEY_VALUE_HEADS, HEAD_SIZE
        ),
        cosine_table[:, None, :],
        sine_values[:, None, :],
    ).astype(jnp.bfloat16)
    value_matrix_rows = (
        projected_rows[:, head_column_width + key_value_width :]
        .reshape(sequence_length, KEY_VALUE_HEADS, HEAD_SIZE)
        .astype(jnp.bfloat16)
    )
    masked = attention_scores(query_matrix, key_matrix_rows, allowed)
    peak_score = jnp.max(masked, axis=-1, keepdims=True)
    log_total = peak_score + jnp.log(jnp.sum(jnp.exp(masked - peak_score), axis=-1, keepdims=True))
    prob_low = jnp.exp(masked - log_total).astype(jnp.bfloat16)
    attended = jnp.einsum(
        "grtu,ugd->tgrd", prob_low, value_matrix_rows, preferred_element_type=jnp.float32
    )
    attended = attended.reshape(sequence_length, head_column_width).astype(jnp.bfloat16)
    hidden = residual + right_trans(attended, out_w)
    normed_two = norm_rows(hidden, gain_row[model_width:].astype(jnp.float32)).astype(jnp.bfloat16)
    gate_proj = matmul(normed_two, ffn_w[0])
    upward = matmul(normed_two, ffn_w[1])
    active = (jax.nn.silu(gate_proj) * upward).astype(jnp.bfloat16)
    output = hidden + right_trans(active, ffn_w[2])
    saved_state = (
        residual,
        normed,
        query_matrix,
        key_matrix_rows,
        value_matrix_rows,
        log_total,
        attended,
        hidden,
        normed_two,
        gate_proj,
        upward,
        active,
    )
    return (output, saved_state)


def layer_backward(
    grad_out, saved_state, qkv_w, out_w, ffn_w, gain_row, cosine_table, sine_values, allowed
):
    (
        residual,
        normed,
        query_matrix,
        key_matrix_rows,
        value_matrix_rows,
        log_total,
        attended,
        hidden,
        normed_two,
        gate_proj,
        upward,
        active,
    ) = saved_state
    sequence_length, model_width = residual.shape
    head_column_width = QUERY_HEADS * HEAD_SIZE
    key_value_width = KEY_VALUE_HEADS * HEAD_SIZE
    query_group_count = QUERY_HEADS // KEY_VALUE_HEADS
    branch_grad = grad_out.astype(jnp.bfloat16)
    active_grad = matmul(branch_grad, ffn_w[2])
    _, pull_back = jax.vjp(lambda gate_in, up_in: jax.nn.silu(gate_in) * up_in, gate_proj, upward)
    gate_grad, up_grad = pull_back(active_grad)
    gate_grad = gate_grad.astype(jnp.bfloat16)
    up_grad = up_grad.astype(jnp.bfloat16)
    normed_two_grad = right_trans(gate_grad, ffn_w[0]) + right_trans(up_grad, ffn_w[1])
    _, pull_back = jax.vjp(norm_rows, hidden, gain_row[model_width:].astype(jnp.float32))
    hidden_part, gain_two_grad = pull_back(normed_two_grad)
    hidden_grad = grad_out + hidden_part
    mixed_grad = hidden_grad.astype(jnp.bfloat16)
    attended_grad = (
        matmul(mixed_grad, out_w)
        .reshape(sequence_length, KEY_VALUE_HEADS, query_group_count, HEAD_SIZE)
        .astype(jnp.bfloat16)
    )
    prob_full = jnp.exp(attention_scores(query_matrix, key_matrix_rows, allowed) - log_total)
    prob_low = prob_full.astype(jnp.bfloat16)
    value_grad = jnp.einsum(
        "grtu,tgrd->ugd", prob_low, attended_grad, preferred_element_type=jnp.float32
    )
    prob_grad = jnp.einsum(
        "tgrd,ugd->grtu", attended_grad, value_matrix_rows, preferred_element_type=jnp.float32
    )
    scores_grad = (
        prob_full * (prob_grad - jnp.sum(prob_grad * prob_full, axis=-1, keepdims=True))
    ).astype(jnp.bfloat16)
    query_grad = jnp.einsum(
        "grtu,ugd->tgrd", scores_grad, key_matrix_rows, preferred_element_type=jnp.float32
    ) * HEAD_SIZE ** (-0.5)
    key_grad = jnp.einsum(
        "grtu,tgrd->ugd", scores_grad, query_matrix, preferred_element_type=jnp.float32
    ) * HEAD_SIZE ** (-0.5)
    _, pull_back = jax.vjp(
        lambda rows: rotary_apply(
            rows, cosine_table[:, None, None, :], sine_values[:, None, None, :]
        ),
        query_grad,
    )
    (query_grad,) = pull_back(query_grad)
    _, pull_back = jax.vjp(
        lambda rows: rotary_apply(rows, cosine_table[:, None, :], sine_values[:, None, :]), key_grad
    )
    (key_grad,) = pull_back(key_grad)
    qkv_grad = jnp.concatenate(
        [
            query_grad.reshape(sequence_length, head_column_width),
            key_grad.reshape(sequence_length, key_value_width),
            value_grad.reshape(sequence_length, key_value_width),
        ],
        axis=1,
    ).astype(jnp.bfloat16)
    normed_grad = right_trans(qkv_grad, qkv_w)
    _, pull_back = jax.vjp(norm_rows, residual, gain_row[:model_width].astype(jnp.float32))
    input_part, gain_one_grad = pull_back(normed_grad)
    input_grad = hidden_grad + input_part
    pieces = (
        normed,
        qkv_grad,
        mixed_grad,
        attended,
        normed_two,
        gate_grad,
        up_grad,
        branch_grad,
        active,
    )
    return (input_grad, pieces, jnp.concatenate([gain_one_grad, gain_two_grad]))


def owner_rows_maker(piece_group, owners):
    joined = tuple(
        (jnp.concatenate([pieces[member] for pieces in piece_group], axis=0) for member in range(9))
    )
    normed, qkv_grad, mixed_grad, attended, normed_two, gate_grad, up_grad, branch_grad, active = (
        joined
    )
    token_count = normed.shape[0]
    qkv_cols = qkv_grad.shape[1]
    out_cols = attended.shape[1]
    qkv_padded = jnp.concatenate(
        [qkv_grad, jnp.zeros((token_count, out_cols), jnp.bfloat16)], axis=1
    )
    out_padded = jnp.concatenate(
        [jnp.zeros((token_count, qkv_cols), jnp.bfloat16), attended], axis=1
    )
    attn_share = (qkv_cols + out_cols) // owners
    ffn_share = gate_grad.shape[1] // owners
    owner_width = attn_share + 3 * ffn_share

    def one_owner(owner):
        attn_first = lax.dynamic_slice_in_dim(qkv_padded, owner * attn_share, attn_share, 1)
        attn_second = lax.dynamic_slice_in_dim(out_padded, owner * attn_share, attn_share, 1)
        attn_rows = left_trans(attn_first, normed) + left_trans(attn_second, mixed_grad)
        gate_rows = left_trans(
            lax.dynamic_slice_in_dim(gate_grad, owner * ffn_share, ffn_share, 1), normed_two
        )
        up_rows = left_trans(
            lax.dynamic_slice_in_dim(up_grad, owner * ffn_share, ffn_share, 1), normed_two
        )
        down_rows = left_trans(
            lax.dynamic_slice_in_dim(active, owner * ffn_share, ffn_share, 1), branch_grad
        )
        return jnp.concatenate([attn_rows, gate_rows, up_rows, down_rows], axis=0)

    def owner_rows(start, count):
        block_total = count // owner_width
        first_owner = start // owner_width
        owner_list = jnp.arange(block_total, dtype=jnp.int32)
        stacked = lax.map(one_owner, owner_list)
        return stacked.reshape(count, stacked.shape[-1])

    return (owner_rows, owner_width, attn_share, ffn_share)


def unpack_shard(shard, attn_share, ffn_share):
    attention_shard = shard[:attn_share].T[None]
    gate_part = shard[attn_share : attn_share + ffn_share].T
    up_part = shard[attn_share + ffn_share : attn_share + 2 * ffn_share].T
    down_part = shard[attn_share + 2 * ffn_share :].T
    return (attention_shard, jnp.stack([gate_part, up_part, down_part])[None])


def pick_section(leading, first_tree, second_tree):
    return jax.tree.map(
        lambda one_val, two_val: jnp.where(leading, one_val, two_val), first_tree, second_tree
    )


def local(edge_data, segment_ids, attn_weight, ffn_weight, gains):
    micro_count = segment_ids.shape[0]
    owners = lax.axis_size("dp")
    split_at = QUERY_HEADS * HEAD_SIZE + 2 * KEY_VALUE_HEADS * HEAD_SIZE
    leading = lax.axis_index("section") == 0
    table_list = [block_tables(segment_ids[mb_num]) for mb_num in range(micro_count)]
    gathered = (
        lax.all_gather(attn_weight, "dp", axis=2, tiled=True),
        lax.all_gather(ffn_weight, "dp", axis=3, tiled=True),
        lax.all_gather(gains, "dp", axis=1, tiled=True),
    )
    qkv_w = gathered[0][0][:, :split_at]
    out_w = gathered[0][0][:, split_at:]
    ffn_w, gain_row = (gathered[1][0], gathered[2][0])
    received = jnp.zeros_like(edge_data[0, 0])
    saved_list = []
    output_list = []
    for tick_num in range(micro_count + 1):
        own_input = edge_data[0, min(tick_num, micro_count - 1)]
        layer_in = jnp.where(leading, own_input, received)
        cosine_table, sine_values, allowed = pick_section(
            leading, table_list[min(tick_num, micro_count - 1)], table_list[max(tick_num - 1, 0)]
        )
        output, saved_state = layer_forward(
            layer_in, qkv_w, out_w, ffn_w, gain_row, cosine_table, sine_values, allowed
        )
        saved_list.append(saved_state)
        output_list.append(output)
        if tick_num < micro_count:
            received = passed_along(output.astype(jnp.bfloat16), "section", 1)
    back_weights = (
        lax.all_gather(attn_weight, "dp", axis=2, tiled=True),
        lax.all_gather(ffn_weight, "dp", axis=3, tiled=True),
        lax.all_gather(gains, "dp", axis=1, tiled=True),
    )
    qkv_w = back_weights[0][0][:, :split_at]
    out_w = back_weights[0][0][:, split_at:]
    ffn_w, gain_row = (back_weights[1][0], back_weights[2][0])
    grad_received = jnp.zeros_like(edge_data[0, 0])
    piece_list = []
    input_grad_list = []
    gain_total = jnp.zeros(gain_row.shape, jnp.float32)
    for tick_num in range(micro_count + 1):
        saved_state = pick_section(
            leading, saved_list[max(tick_num - 1, 0)], saved_list[min(tick_num + 1, micro_count)]
        )
        cosine_table, sine_values, allowed = pick_section(
            leading, table_list[max(tick_num - 1, 0)], table_list[min(tick_num, micro_count - 1)]
        )
        cotangent = edge_data[1, min(tick_num, micro_count - 1)]
        incoming = jnp.where(leading, grad_received, cotangent).astype(jnp.float32)
        is_valid = jnp.where(leading, tick_num >= 1, tick_num < micro_count)
        incoming = jnp.where(is_valid, incoming, 0.0)
        input_grad, pieces, gain_grad = layer_backward(
            incoming, saved_state, qkv_w, out_w, ffn_w, gain_row, cosine_table, sine_values, allowed
        )
        input_grad_list.append(input_grad)
        gain_total = gain_total + gain_grad
        piece_list.append(pieces)
        if tick_num < micro_count:
            grad_received = passed_along(input_grad.astype(jnp.bfloat16), "section", -1)
    owner_rows, owner_width, attn_share, ffn_share = owner_rows_maker(piece_list, owners)
    total_shard = lax.psum_scatter(
        owner_rows(jnp.int32(0), owner_width * lax.axis_size("dp")),
        "dp",
        scatter_dimension=0,
        tiled=True,
    )
    attention_shard, ffn_shard = unpack_shard(total_shard, attn_share, ffn_share)
    gain_shard = lax.psum_scatter(gain_total[None], "dp", scatter_dimension=1, tiled=True)
    edge_out = jnp.stack(
        [
            jnp.where(leading, input_grad_list[mb_num + 1], output_list[mb_num + 1])
            for mb_num in range(micro_count)
        ]
    ).astype(jnp.bfloat16)
    return (edge_out[None], attention_shard, ffn_shard, gain_shard)


def solution(mesh):
    in_specs = (
        P("section", None, "dp", None),
        P(None, "dp"),
        P("section", None, "dp"),
        P("section", None, None, "dp"),
        P("section", "dp"),
    )
    out_specs = (
        P("section", None, "dp", None),
        P("section", None, "dp"),
        P("section", None, None, "dp"),
        P("section", "dp"),
    )
    return jax.shard_map(local, mesh=mesh, in_specs=in_specs, out_specs=out_specs, check_vma=False)
```

profile of v0, /device:TPU:0, one launch (start us, length us, event | category | flops | bytes accessed | tf_op | source)
XLA Modules:
  0.0 897.4 jit_solution(8501034763040781893)
XLA Ops:
  11.6 35.6 %all-reduce.14 = bf16[1920]{0:T(1024)(128)(2,1)S(1)} all-reduce(bf16[1920]{0:T(1024)(128)(2,1)S(1)} %dynamic-update-slice), channel_id=1, replica_groups=mesh['section'=2,'dp'=16] {'dp'}, use_global_device_ids=true, to_apply=%add.14 | all-reduce | flops 1920 | bytes 7680
  50.9 17.9 %all-gather.5.cloned.1.call-done = bf16[1,960,2560]{1,2,0:T(8,128)(2,1)} async-done(((bf16[1,960,160]{1,2,0:T(8,128)(2,1)}), bf16[1,960,2560]{1,2,0:T(8,128)(2,1)}) %all-gather.5.cloned.1.call-update) | async-done | bytes 4915216 | tf_op jit(solution)/shard_map/all_gather | solution.py:287
  68.8 3.1 fusion.55
  76.6 113.0 %all-gather.3.cloned.1.call-done = bf16[1,3,960,2560]{2,3,1,0:T(8,128)(2,1)} async-done(((bf16[1,3,960,160]{2,3,1,0:T(8,128)(2,1)}), bf16[1,3,960,2560]{2,3,1,0:T(8,128)(2,1)}) %all-gather.3.cloned.1.call-update) | async-done | bytes 14745616 | tf_op jit(solution)/shard_map/all_gather | solution.py:312
  189.6 4.2 fusion.41
  193.8 5.3 multiply_convert_fusion.5
  199.1 3.6 fusion.92
  202.7 3.6 collective-permute-start
  210.0 3.1 fusion.53
  219.0 4.3 fusion.40
  223.4 5.4 broadcast_select_fusion.2
  228.8 4.6 fusion.112
  243.0 4.2 fusion.90
  247.2 4.4 collective-permute-start.2
  251.6 2.5 collective-permute-done.2
  254.1 4.1 multiply_reduce_fusion.8
  263.3 2.9 multiply_reduce_fusion.16
  273.9 4.3 fusion.38
  278.3 4.6 broadcast_select_fusion.1
  286.3 4.3 fusion.91
  293.0 4.5 fusion.115
  309.9 3.4 multiply_reduce_fusion.6
  317.5 4.4 collective-permute-done.3
  321.9 4.7 fusion.118
  326.7 3.8 fusion.30
  330.6 4.2 multiply_reduce_fusion.3
  345.3 5.3 fusion.60
  350.6 2.8 multiply_reduce_fusion.4
  354.8 133.8 %while.10 = (s32[]{:T(128)}, f32[16,640,960]{2,1,0:T(8,128)}, s32[16]{0:T(128)S(1)}, bf16[192,2560]{0,1:T(8,128)(2,1)}, bf16[192,960]{1,0:T(8,128)(2,1)S(1)}, /*...) while((s32[]{:T(128)}, f32[16,640,960]{2,1,0:T(8,128)}, ...), condition=%wide.region_30.31_spmd, body=%wide.region_29.30_spmd.sunk | while | flops 296908800 | bytes 11109091 | solution.py:260
  489.5 30.0 %all-reduce.15 = f32[1,1920]{1,0:T(1,128)S(1)} all-reduce(f32[1,1920]{1,0:T(1,128)S(1)} %fusion.191), channel_id=3, replica_groups=mesh['section'=2,'dp'=16] {'dp'}, use_global_device_ids=true, to_apply=%region_38.39.clone | all-reduce | flops 1920 | bytes 15360
  520.9 365.7 %reduce-scatter.3.cloned.1.call-done = f32[640,960]{1,0:T(8,128)} async-done(((f32[10240,960]{1,0:T(8,128)}), f32[640,960]{1,0:T(8,128)}) %reduce-scatter.3.cloned.1.call-update) | async-done | bytes 2457616 | tf_op jit(solution)/shard_map/reduce_scatter | solution.py:342
  886.5 2.7 slice_bitcast_fusion.37
  (533 shorter events, 202.3 us)
Async XLA Ops:
  7.2 61.7 %all-gather.5.cloned.1.call-start = ((), (), s32[]{:S(2)}) async-start(), calls=%async_computation.2 | async-start | bytes 5570560 | tf_op jit(solution)/shard_map/all_gather | solution.py:287
  7.9 181.7 %all-gather.3.cloned.1.call-start = ((), (), s32[]{:S(2)}) async-start(), calls=%async_computation.1 | async-start | bytes 16711680 | tf_op jit(solution)/shard_map/all_gather | solution.py:312
  8.6 877.9 %reduce-scatter.3.cloned.1.call-start = ((), (), s32[]{:S(2)}) async-start(), calls=%async_computation.3 | async-start | bytes 44564480 | tf_op jit(solution)/shard_map/reduce_scatter | solution.py:342
  49.2 23.0 %copy-start.73 = (f32[64]{0:T(128)}, f32[64]{0:T(128)S(1)}, u32[]{:S(2)}) copy-start(f32[64]{0:T(128)S(1)} %add_rsqrt_fusion.5) | copy-start | bytes 772
  49.3 160.7 %copy-start.58 = (f32[1,960]{1,0:T(1,128)}, f32[1,960]{1,0:T(1,128)S(1)}, u32[]{:S(2)}) copy-start(f32[1,960]{1,0:T(1,128)S(1)} %get-tuple-element.217) | copy-start | bytes 11524
  49.3 223.8 %copy-start.55 = (f32[1,960]{1,0:T(1,128)}, f32[1,960]{1,0:T(1,128)S(1)}, u32[]{:S(2)}) copy-start(f32[1,960]{1,0:T(1,128)S(1)} %get-tuple-element.216) | copy-start | bytes 11524
  50.9 209.8 %copy-start.15 = (f32[64,32]{1,0:T(8,128)}, f32[64,32]{1,0:T(8,128)S(1)}, u32[]{:S(2)}) copy-start(f32[64,32]{1,0:T(8,128)S(1)} %get-tuple-element.224) | copy-start | bytes 24580
  50.9 209.8 %copy-start.18 = (f32[64,32]{1,0:T(8,128)}, f32[64,32]{1,0:T(8,128)S(1)}, u32[]{:S(2)}) copy-start(f32[64,32]{1,0:T(8,128)S(1)} %get-tuple-element.225) | copy-start | bytes 24580
  76.6 141.7 %copy-start.83 = (f32[64]{0:T(128)}, f32[64]{0:T(128)S(1)}, u32[]{:S(2)}) copy-start(f32[64]{0:T(128)S(1)} %add_rsqrt_fusion.4) | copy-start | bytes 772
  199.1 14.0 %copy-start.101 = (bf16[64,2560]{1,0:T(8,128)(2,1)}, bf16[64,2560]{1,0:T(8,128)(2,1)S(1)}, u32[]{:S(2)}) copy-start(bf16[64,2560]{1,0:T(8,128)(2,1)S(1)} %get-tuple-element.238) | copy-start | bytes 983044
  202.7 6.5 collective-permute-start
  207.8 32.0 %copy-start.21 = (bf16[64,5,64]{2,0,1:T(8,128)(2,1)}, bf16[64,5,64]{2,0,1:T(8,128)(2,1)S(1)}, u32[]{:S(2)}) copy-start(bf16[64,5,64]{2,0,1:T(8,128)(2,1)S(1)} %copy.141) | copy-start | bytes 122884
  215.9 17.6 %slice-start.2 = ((s8[15728640]{0:T(1024)(128)(4,1)}), s8[4194304]{0:T(1024)(128)(4,1)S(1)}, s32[]{:S(2)}) async-start(s8[15728640]{0:T(1024)(128)(4,1)} %bitcast.493), calls=%async_computation.6 | async-start | bytes 8388608
  219.0 14.5 %slice-start.3 = ((s8[15728640]{0:T(1024)(128)(4,1)}), s8[4194304]{0:T(1024)(128)(4,1)S(1)}, s32[]{:S(2)}) async-start(s8[15728640]{0:T(1024)(128)(4,1)} %bitcast.493), calls=%async_computation.7 | async-start | bytes 8388608
  241.2 12.9 %copy-start.40 = (bf16[5,64,64]{2,1,0:T(8,128)(2,1)}, bf16[5,64,64]{2,1,0:T(8,128)(2,1)S(1)}, u32[]{:S(2)}) copy-start(bf16[5,64,64]{2,1,0:T(8,128)(2,1)S(1)} %fusion.99) | copy-start | bytes 122884
  242.6 15.6 %copy-start.13 = (bf16[64,5,3,64]{0,3,2,1:T(8,128)(2,1)}, bf16[64,5,3,64]{0,3,2,1:T(8,128)(2,1)S(1)}, u32[]{:S(2)}) copy-start(bf16[64,5,3,64]{0,3,2,1:T(8,128)(2,1)S(1)} %copy.148) | copy-start | bytes 368644
  243.0 15.2 %copy-start.42 = (bf16[64,5,64]{0,2,1:T(8,128)(2,1)}, bf16[64,5,64]{0,2,1:T(8,128)(2,1)S(1)}, u32[]{:S(2)}) copy-start(bf16[64,5,64]{0,2,1:T(8,128)(2,1)S(1)} %copy.152) | copy-start | bytes 122884
  243.0 15.2 %slice-start = ((s8[5242880]{0:T(1024)(128)(4,1)}), s8[4194304]{0:T(1024)(128)(4,1)S(1)}, s32[]{:S(2)}) async-start(s8[5242880]{0:T(1024)(128)(4,1)} %bitcast.421), calls=%async_computation.4 | async-start | bytes 8388608
  243.0 15.2 %slice-start.1 = ((s8[5242880]{0:T(1024)(128)(4,1)}), s8[1048576]{0:T(1024)(128)(4,1)S(1)}, s32[]{:S(2)}) async-start(s8[5242880]{0:T(1024)(128)(4,1)} %bitcast.421), calls=%async_computation.5 | async-start | bytes 2097152
  247.2 6.9 collective-permute-start.2
  260.8 44.0 %copy-start.1 = (bf16[64,5,64]{2,0,1:T(8,128)(2,1)}, bf16[64,5,64]{2,0,1:T(8,128)(2,1)S(1)}, u32[]{:S(2)}) copy-start(bf16[64,5,64]{2,0,1:T(8,128)(2,1)S(1)} %pad_maximum_fusion.13) | copy-start | bytes 122884
  260.8 12.3 %copy-start.84 = (f32[64]{0:T(128)S(1)}, f32[64]{0:T(128)}, u32[]{:S(2)}) copy-start(f32[64]{0:T(128)} %copy-done.83) | copy-start | bytes 772
  266.3 16.6 %copy-start.7 = (f32[64,960]{1,0:T(8,128)}, f32[64,960]{1,0:T(8,128)S(1)}, u32[]{:S(2)}) copy-start(f32[64,960]{1,0:T(8,128)S(1)} %get-tuple-element.250) | copy-start | bytes 737284
  266.3 24.4 %copy-start.87 = (f32[64]{0:T(128)}, f32[64]{0:T(128)S(1)}, u32[]{:S(2)}) copy-start(f32[64]{0:T(128)S(1)} %get-tuple-element.197) | copy-start | bytes 772
  270.5 20.7 %collective-permute-start.1 = (bf16[64,960]{1,0:T(8,128)(2,1)}, bf16[64,960]{1,0:T(8,128)(2,1)}, u32[]{:S(2)}, u32[]{:S(2)}) collective-permute-start(bf16[64,960]{1,0:T(8,128)(2,1)} %fusion.136), channel_id=1, source_target_pairs={{16,0},{17,1},{18,2},{19,3},{20,4},{21,5},{22,6},{23,7},{24,8},{25... | collective-permute-start | bytes 368648 | tf_op jit(solution)/shard_map/ppermute | solution.py:20
  271.8 28.5 %copy-start.79 = (f32[64]{0:T(128)}, f32[64]{0:T(128)S(1)}, u32[]{:S(2)}) copy-start(f32[64]{0:T(128)S(1)} %fusion.194) | copy-start | bytes 772
  273.9 23.6 %slice-start.6 = ((s8[15728640]{0:T(1024)(128)(4,1)}), s8[4194304]{0:T(1024)(128)(4,1)S(1)}, s32[]{:S(2)}) async-start(s8[15728640]{0:T(1024)(128)(4,1)} %bitcast.495), calls=%async_computation.10 | async-start | bytes 8388608
  278.2 14.7 %copy-start.100 = (f32[64,2560]{1,0:T(8,128)}, f32[64,2560]{1,0:T(8,128)S(1)}, u32[]{:S(2)}) copy-start(f32[64,2560]{1,0:T(8,128)S(1)} %fusion.38) | copy-start | bytes 1966084
  278.3 19.2 %slice-start.7 = ((s8[15728640]{0:T(1024)(128)(4,1)}), s8[4194304]{0:T(1024)(128)(4,1)S(1)}, s32[]{:S(2)}) async-start(s8[15728640]{0:T(1024)(128)(4,1)} %bitcast.495), calls=%async_computation.11 | async-start | bytes 8388608
  284.4 13.1 %slice-start.8 = ((s8[15728640]{0:T(1024)(128)(4,1)}), s8[4194304]{0:T(1024)(128)(4,1)S(1)}, s32[]{:S(2)}) async-start(s8[15728640]{0:T(1024)(128)(4,1)} %bitcast.495), calls=%async_computation.12 | async-start | bytes 8388608
  314.4 7.4 collective-permute-start.3
  488.7 31.4 %copy-start.39 = (bf16[1,1,64,960]{3,2,1,0:T(8,128)(2,1)S(1)}, bf16[1,1,64,960]{3,2,1,0:T(8,128)(2,1)}, u32[]{:S(2)}) copy-start(bf16[1,1,64,960]{3,2,1,0:T(8,128)(2,1)} %get-tuple-element.140) | copy-start | bytes 368644
  (92 other events, 563.2 us)
Sparse Core Ops, SparseCore 0:
  10.3 58.5 all-gather.4
  71.1 118.4 all-gather.2
  488.8 397.6 reduce-scatter.2
where the time goes:
time: 906 us; the launch traced here: 897 us
  waiting for transfers between devices  506 us (56%)
  matrix products  192 us (21%)
  other arithmetic  67 us (7%)
  blocking collectives  65.5 us (7%)
  local copies, waits for them, and re-layouts  27.3 us (3%)
  between operations  17.5 us (2%)
  loops' own time  11.2 us (1%)
  starting transfers between devices  10.8 us (1%)
    reduce_scatter x1, waiting for transfers between devices, local(): lax.psum_scatter(owner_rows(jnp.int32(0), owner_width * lax.axis_size('dp...  366 us
    all_gather x1, waiting for transfers between devices, local(): lax.all_gather(ffn_weight, 'dp', axis=3, tiled=True)  113 us
    dot_general x80, matrix products, left_trans(): lax.dot_general(left_op, right_op, contract_first, preferred_element_type...  83.9 us
    unnamed x2, blocking collectives  65.5 us
    dot_general x15, matrix products, matmul(): return jnp.dot(left_op, right_op, preferred_element_type=jnp.float32)  56.3 us
    dot_general x15, matrix products, right_trans(): lax.dot_general(left_op, right_op, contract_last, preferred_element_type=...  43.2 us
    dynamic_update_slice x16, other arithmetic, owner_rows(): stacked = lax.map(one_owner, owner_list)  29.5 us
  transfers between devices with their start and end apart: 7, of which 6 were waited for; matrix products, arithmetic and copies ran while one was open for 4% of the time, Pallas kernels for 0%

commit v1 on v0

v1 whole, which is shorter than its diff:
```python
import jax
import jax.numpy as jnp
from jax import lax
from jax.sharding import PartitionSpec as P

QUERY_HEADS = 15
KEY_VALUE_HEADS = 5
GROUP = QUERY_HEADS // KEY_VALUE_HEADS
HEAD_SIZE = 64
BLOCK = 64
QCOLS = QUERY_HEADS * HEAD_SIZE
KVCOLS = KEY_VALUE_HEADS * HEAD_SIZE
SPLIT = QCOLS + 2 * KVCOLS
SCALE = HEAD_SIZE ** (-0.5)
EPS = 1e-05
THETA = 100000.0
BF = jnp.bfloat16
F32 = jnp.float32


def matmul(a, b):
    return jnp.dot(a, b, preferred_element_type=F32)


def right_trans(a, b):
    return lax.dot_general(a, b, (((1,), (1,)), ((), ())), preferred_element_type=F32)


def left_trans(a, b):
    return lax.dot_general(a, b, (((0,), (0,)), ((), ())), preferred_element_type=F32)


def inv_rms(x):
    return lax.rsqrt(jnp.mean(x * x, axis=-1, keepdims=True) + EPS)


def rope(x, cos, sin):
    half = HEAD_SIZE // 2
    a = x[..., :half]
    b = x[..., half:]
    return jnp.concatenate([a * cos - b * sin, b * cos + a * sin], axis=-1)


def tables(segment_ids):
    seg = segment_ids.reshape(-1)
    tokens = seg.shape[0]
    idx = jnp.arange(tokens, dtype=jnp.int32)
    seg = seg + BLOCK * (idx // BLOCK)
    same = seg[:, None] == seg[None, :]
    start = jnp.min(jnp.where(same, idx[None, :], tokens), axis=-1)
    pos = (idx - start).astype(F32)
    half = HEAD_SIZE // 2
    freq = THETA ** (-(2.0 * jnp.arange(half, dtype=F32)) / HEAD_SIZE)
    ang = pos[:, None] * freq
    allowed = same & (idx[:, None] >= idx[None, :])
    return jnp.cos(ang), jnp.sin(ang), allowed


def scores(q, k, allowed):
    s = jnp.einsum("grtd,gud->grtu", q, k, preferred_element_type=F32) * SCALE
    return jnp.where(allowed, s, -1000000000.0)


def forward(u, w, tabs):
    qkv_t, out_t, gate_t, up_t, down_t, g1, g2 = w
    cos, sin, allowed = tabs
    rows = u.shape[0]
    n = (u * inv_rms(u) * g1).astype(BF)
    proj = right_trans(n, qkv_t)
    heads = proj.reshape(rows, -1, HEAD_SIZE).transpose(1, 0, 2)
    turned = rope(heads[: QUERY_HEADS + KEY_VALUE_HEADS], cos, sin).astype(BF)
    q = turned[:QUERY_HEADS].reshape(KEY_VALUE_HEADS, GROUP, rows, HEAD_SIZE)
    k = turned[QUERY_HEADS:]
    v = heads[QUERY_HEADS + KEY_VALUE_HEADS :].astype(BF)
    s = scores(q, k, allowed)
    peak = jnp.max(s, axis=-1, keepdims=True)
    lse = peak + jnp.log(jnp.sum(jnp.exp(s - peak), axis=-1, keepdims=True))
    p = jnp.exp(s - lse).astype(BF)
    o = jnp.einsum("grtu,gud->grtd", p, v, preferred_element_type=F32)
    o = o.astype(BF).reshape(QUERY_HEADS, rows, HEAD_SIZE).transpose(1, 0, 2).reshape(rows, QCOLS)
    h1 = u + matmul(o, out_t)
    m = (h1 * inv_rms(h1) * g2).astype(BF)
    gate = right_trans(m, gate_t)
    up = right_trans(m, up_t)
    act = (gate * jax.nn.sigmoid(gate) * up).astype(BF)
    out = h1 + matmul(act, down_t)
    return out, (u, n, q, k, v, lse, o, h1, m, gate, up, act)


def norm_back(dy, x, g):
    r = inv_rms(x)
    dg = dy * g
    dx = r * dg - x * (r * r * r) * jnp.mean(dg * x, axis=-1, keepdims=True)
    return dx, jnp.sum(dy * x * r, axis=0)


def backward(e, saved, w, tabs):
    u, n, q, k, v, lse, o, h1, m, gate, up, act = saved
    qkv_t, out_t, gate_t, up_t, down_t, g1, g2 = w
    cos, sin, allowed = tabs
    rows = u.shape[0]
    eb = e.astype(BF)
    da = right_trans(eb, down_t)
    sg = jax.nn.sigmoid(gate)
    dgate = (da * up * sg * (1.0 + gate * (1.0 - sg))).astype(BF)
    dup = (da * (gate * sg)).astype(BF)
    dm = matmul(dgate, gate_t) + matmul(dup, up_t)
    dx, gain2 = norm_back(dm, h1, g2)
    dh1 = e + dx
    dz = dh1.astype(BF)
    do = right_trans(dz, out_t).astype(BF)
    do = do.reshape(rows, QUERY_HEADS, HEAD_SIZE).transpose(1, 0, 2)
    do = do.reshape(KEY_VALUE_HEADS, GROUP, rows, HEAD_SIZE)
    p = jnp.exp(scores(q, k, allowed) - lse)
    dv = jnp.einsum("grtu,grtd->gud", p.astype(BF), do, preferred_element_type=F32)
    dp = jnp.einsum("grtd,gud->grtu", do, v, preferred_element_type=F32)
    ds = (p * (dp - jnp.sum(dp * p, axis=-1, keepdims=True))).astype(BF)
    dq = jnp.einsum("grtu,gud->grtd", ds, k, preferred_element_type=F32) * SCALE
    dk = jnp.einsum("grtu,grtd->gud", ds, q, preferred_element_type=F32) * SCALE
    dq = dq.reshape(QUERY_HEADS, rows, HEAD_SIZE)
    dqk = rope(jnp.concatenate([dq, dk], axis=0), cos, -sin)
    dproj = jnp.concatenate([dqk, dv], axis=0).astype(BF).transpose(1, 0, 2).reshape(rows, SPLIT)
    dn = matmul(dproj, qkv_t)
    dx, gain1 = norm_back(dn, u, g1)
    return dh1 + dx, (eb, dgate, dup, dz, dproj), jnp.concatenate([gain1, gain2])


def to_owners(columns, owners):
    rows, cols = columns.shape
    share = cols // owners
    blocks = columns.reshape(rows, owners, share).transpose(1, 0, 2)
    return lax.all_to_all(blocks, "dp", 0, 0, tiled=True).reshape(owners * rows, share)


def local(edge_data, segment_ids, attn_weight, ffn_weight, gains):
    owners = lax.axis_size("dp")
    share = attn_weight.shape[2]
    leading = lax.axis_index("section") == 0

    def whole(x):
        return lax.all_gather(x, "dp", axis=0, tiled=True)

    gain_row = whole(gains[0]).astype(F32)
    attn_t = whole(attn_weight[0].T)
    gate_t = whole(ffn_weight[0, 0].T)
    up_t = whole(ffn_weight[0, 1].T)
    down_t = whole(ffn_weight[0, 2].T)
    width = attn_t.shape[1]
    w = (attn_t[:SPLIT], attn_t[SPLIT:], gate_t, up_t, down_t, gain_row[:width], gain_row[width:])
    tabs = tables(segment_ids)
    edge = edge_data[0].reshape(-1, width)

    first_out, _ = forward(edge.astype(F32), w, tabs)
    received = lax.ppermute(first_out.astype(BF), "section", [(0, 1)])
    layer_in = jnp.where(leading, edge, received).astype(F32)
    out, saved = forward(layer_in, w, tabs)
    n, o, m, act = saved[1], saved[6], saved[8], saved[11]
    n_all = whole(n)
    m_all = whole(m)

    sent, _, _ = backward(edge.astype(F32), saved, w, tabs)
    grad_in = lax.ppermute(sent.astype(BF), "section", [(1, 0)])
    e = jnp.where(leading, grad_in, edge).astype(F32)
    du, (eb, dgate, dup, dz, dproj), gain_part = backward(e, saved, w, tabs)
    eb_all = whole(eb)
    dz_all = whole(dz)

    act_own = to_owners(act, owners)
    gate_own = to_owners(dgate, owners)
    up_own = to_owners(dup, owners)
    attn_own = to_owners(jnp.concatenate([dproj, o], axis=1), owners)
    column = lax.axis_index("dp") * share + jnp.arange(share, dtype=jnp.int32)
    attn_grad = jnp.where(
        column < SPLIT, left_trans(n_all, attn_own), left_trans(dz_all, attn_own)
    )
    ffn_grad = jnp.stack(
        [
            left_trans(m_all, gate_own),
            left_trans(m_all, up_own),
            left_trans(eb_all, act_own),
        ]
    )
    gain_grad = lax.psum_scatter(gain_part, "dp", scatter_dimension=0, tiled=True)
    edge_out = jnp.where(leading, du, out).astype(BF).reshape(edge_data.shape[1:])
    return edge_out[None], attn_grad[None], ffn_grad[None], gain_grad[None]


def solution(mesh):
    in_specs = (
        P("section", None, "dp", None),
        P(None, "dp"),
        P("section", None, "dp"),
        P("section", None, None, "dp"),
        P("section", "dp"),
    )
    out_specs = (
        P("section", None, "dp", None),
        P("section", None, "dp"),
        P("section", None, None, "dp"),
        P("section", "dp"),
    )
    return jax.shard_map(local, mesh=mesh, in_specs=in_specs, out_specs=out_specs, check_vma=False)
```

time: 906 us -> 517 us (0.57)
  waiting for transfers between devices: 506 us -> 277 us
  matrix products: 192 us -> 89.1 us
  other arithmetic: 67 us -> 10.5 us
  starting transfers between devices: 10.8 us -> 27.7 us
  local copies, waits for them, and re-layouts: 27.3 us -> 14.6 us
  loops' own time: 11.2 us -> 0 us
    reduce_scatter x1 -> x0, waiting for transfers between devices: 366 us -> none  [local(): lax.psum_scatter(owner_rows(jnp.int32(0), owner_width * lax.axis_size('dp...]
    dot_general x131 -> x36, matrix products: 192 us -> 89.1 us  [the longest x10 33.9 us: matmul(): return jnp.dot(a, b, preferred_element_type=F32)]
    all_gather x2 -> x8, waiting for transfers between devices: 131 us -> 213 us  [whole(): return lax.all_gather(x, 'dp', axis=0, tiled=True)]
    all_to_all x0 -> x4, waiting for transfers between devices: none -> 48.4 us  [to_owners(): lax.all_to_all(blocks, 'dp', 0, 0, tiled=True).reshape(owners * rows, share)]
    dynamic_update_slice x16 -> x0, other arithmetic: 29.5 us -> none  [owner_rows(): stacked = lax.map(one_owner, owner_list)]
    all_to_all x0 -> x4, starting transfers between devices: none -> 22.3 us  [to_owners(): lax.all_to_all(blocks, 'dp', 0, 0, tiled=True).reshape(owners * rows, share)]
    concatenate x13 -> x6, other arithmetic: 12.8 us -> 1.07 us  [the longest x1 0.88 us: local(): attn_own = to_owners(jnp.concatenate([dproj, o], axis=1), owners)]
    another operation x1 -> x0, loops' own time: 11.2 us -> none  [owner_rows(): stacked = lax.map(one_owner, owner_list)]
  transfers between devices with their start and end apart: 7 -> 14, of which waited for: 6 -> 10; matrix products, arithmetic and copies ran while one was open for 4% -> 18% of each run, Pallas kernels for 0% -> 0%
where the time goes in v1:
time: 517 us; the launch traced here: 508 us
  waiting for transfers between devices  277 us (54%)
  matrix products  89.1 us (17%)
  blocking collectives  71.4 us (14%)
  starting transfers between devices  27.7 us (5%)
  between operations  16.9 us (3%)
  local copies, waits for them, and re-layouts  14.6 us (3%)
  other arithmetic  10.5 us (2%)
    all_gather x8, waiting for transfers between devices, whole(): return lax.all_gather(x, 'dp', axis=0, tiled=True)  213 us
    unnamed x2, blocking collectives  71.4 us
    all_to_all x4, waiting for transfers between devices, to_owners(): lax.all_to_all(blocks, 'dp', 0, 0, tiled=True).reshape(owners * rows, share)  48.4 us
    dot_general x10, matrix products, matmul(): return jnp.dot(a, b, preferred_element_type=F32)  33.9 us
    dot_general x9, matrix products, right_trans(): lax.dot_general(a, b, (((1,), (1,)), ((), ())), preferred_element_type=F32)  31.8 us
    all_to_all x4, starting transfers between devices, to_owners(): lax.all_to_all(blocks, 'dp', 0, 0, tiled=True).reshape(owners * rows, share)  22.3 us
    dot_general x5, matrix products, left_trans(): lax.dot_general(a, b, (((0,), (0,)), ((), ())), preferred_element_type=F32)  17.8 us
  transfers between devices with their start and end apart: 14, of which 10 were waited for; matrix products, arithmetic and copies ran while one was open for 18% of the time, Pallas kernels for 0%

profile of v1, /device:TPU:0, one launch (start us, length us, event | category | flops | bytes accessed | tf_op | source)
XLA Modules:
  0.0 507.5 jit_solution(3437838525780481307)
XLA Ops:
  13.9 35.8 %all-reduce = bf16[1920]{0:T(1024)(128)(2,1)S(1)} all-reduce(bf16[1920]{0:T(1024)(128)(2,1)S(1)} %dynamic-update-slice), channel_id=2, replica_groups=mesh['section'=2,'dp'=16] {'dp'}, use_global_device_ids=true, to_apply=%add | all-reduce | flops 1920 | bytes 7680
  53.1 15.8 %all-gather.10.cloned.1.call-done = bf16[2560,960]{1,0:T(8,128)(2,1)} async-done(((bf16[160,960]{1,0:T(8,128)(2,1)}), bf16[2560,960]{1,0:T(8,128)(2,1)}) %all-gather.10.cloned.1.call-update) | async-done | bytes 4915216 | tf_op jit(solution)/shard_map/all_gather | solution.py:141
  73.9 52.2 %all-gather.12.cloned.1.call-done = bf16[2560,960]{1,0:T(8,128)(2,1)} async-done(((bf16[160,960]{1,0:T(8,128)(2,1)}), bf16[2560,960]{1,0:T(8,128)(2,1)}) %all-gather.12.cloned.1.call-update) | async-done | bytes 4915216 | tf_op jit(solution)/shard_map/all_gather | solution.py:141
  126.1 4.6 fusion.67
  130.7 52.6 %all-gather.16.cloned.1.call-done = bf16[2560,960]{1,0:T(8,128)(2,1)} async-done(((bf16[160,960]{1,0:T(8,128)(2,1)}), bf16[2560,960]{1,0:T(8,128)(2,1)}) %all-gather.16.cloned.1.call-update) | async-done | bytes 4915216 | tf_op jit(solution)/shard_map/all_gather | solution.py:141
  183.3 56.5 %all-gather.14.cloned.1.call-done = bf16[2560,960]{1,0:T(8,128)(2,1)} async-done(((bf16[160,960]{1,0:T(8,128)(2,1)}), bf16[2560,960]{1,0:T(8,128)(2,1)}) %all-gather.14.cloned.1.call-update) | async-done | bytes 4915216 | tf_op jit(solution)/shard_map/all_gather | solution.py:141
  239.8 7.4 %fusion.18 = bf16[128,960]{0,1:T(8,128)(2,1)S(1)} fusion(f32[128,960]{0,1:T(8,128)S(1)} %get-tuple-element.42, bf16[2560,960]{1,0:T(8,128)(2,1)} %all-gather.16.cloned.1.call-done, bf16[2560,960]{1,0:T(8,128)(2,1)} %all-gather.14.cloned.1.call-done, f32[128,2560]{1,0:T(8,128)S(1)} %fusion.67, f32[960]{0:T(1024)S(1)} %bitcast.254, f32[128]{0:T(128)S(1)} %add_rsqrt_fusion.3), kind=kOutput, calls=%fused_computation.44 | convolution fusion | flops 1260871680 | bytes 11882752 | tf_op jit(solution)/shard_map/dot_general | solution.py:22
  247.2 3.4 collective-permute-start
  250.6 5.6 %collective-permute-done = bf16[128,960]{0,1:T(8,128)(2,1)S(1)} collective-permute-done((bf16[128,960]{0,1:T(8,128)(2,1)S(1)}, bf16[128,960]{0,1:T(8,128)(2,1)S(1)}, u32[]{:S(2)}, u32[]{:S(2)}) %collective-permute-start) | collective-permute-done | bytes 245792 | tf_op jit(solution)/shard_map/ppermute | solution.py:154
  257.4 3.0 fusion.101
  266.9 4.5 fusion.107
  271.4 4.6 fusion.109
  276.0 4.9 fusion.108
  291.8 8.0 %collective-permute-done.1 = bf16[128,960]{0,1:T(8,128)(2,1)S(1)} collective-permute-done((bf16[128,960]{0,1:T(8,128)(2,1)S(1)}, bf16[128,960]{0,1:T(8,128)(2,1)S(1)}, u32[]{:S(2)}, u32[]{:S(2)}) %collective-permute-start.1) | collective-permute-done | bytes 245792 | tf_op jit(solution)/shard_map/ppermute | solution.py:162
  300.8 6.4 %multiply_convert_fusion.1 = (bf16[128,2560]{1,0:T(8,128)(2,1)S(1)}, bf16[128,2560]{1,0:T(8,128)(2,1)S(1)}, bf16[128,2560]{1,0:T(8,128)(2,1)}) fusion(f32[128,2560]{1,0:T(8,128)} %copy-done.10, f32[128,2560]{1,0:T(8,128)} %copy-done.11, bf16[128,960]{0,1:T(8,128)(2,1)} %broadcast_select_fusion, bf16[2560,960]{1,0:T(8,128)(2,1)} %all-gather.16.cloned.1.call-done), kind=kOutput, calls=%fused_computation.8 | convolution fusion | flops 634060800 | bytes 9748480 | tf_op jit(solution)/shard_map/dot_general | solution.py:26
  307.1 5.2 %fusion.110 = f32[128,960]{0,1:T(8,128)S(1)} fusion(bf16[128,2560]{1,0:T(8,128)(2,1)S(1)} %get-tuple-element.15, bf16[2560,960]{1,0:T(8,128)(2,1)} %all-gather.12.cloned.1.call-done), kind=kOutput, calls=%fused_computation.205 | convolution fusion | flops 629145600 | bytes 6062080 | tf_op jit(solution)/shard_map/dot_general | solution.py:22
  312.3 4.4 multiply_reduce_fusion.2
  323.5 4.4 all-to-all-start
  330.1 19.6 %all-to-all-done = bf16[16,128,160]{1,2,0:T(8,128)(2,1)} async-done(((bf16[16,128,160]{1,2,0:T(8,128)(2,1)}), bf16[16,128,160]{1,2,0:T(8,128)(2,1)}, u32[]{:S(2)}, u32[]{:S(2)}) %all-to-all-start) | async-done | bytes 655392 | tf_op jit(solution)/shard_map/all_to_all | solution.py:132
  349.6 4.7 all-to-all-start.2
  356.5 22.7 %all-to-all-done.2 = bf16[16,128,160]{1,2,0:T(8,128)(2,1)} async-done(((bf16[16,128,160]{1,2,0:T(8,128)(2,1)}), bf16[16,128,160]{1,2,0:T(8,128)(2,1)}, u32[]{:S(2)}, u32[]{:S(2)}) %all-to-all-start.2) | async-done | bytes 655392 | tf_op jit(solution)/shard_map/all_to_all | solution.py:132
  379.2 9.6 %all-to-all-start.1 = ((bf16[16,128,160]{1,2,0:T(8,128)(2,1)}), bf16[16,128,160]{1,2,0:T(8,128)(2,1)}, u32[]{:S(2)}, u32[]{:S(2)}) async-start(bf16[16,128,160]{1,2,0:T(8,128)(2,1)} %bitcast.230), calls=%async_computation.1 | async-start | bytes 1310720 | tf_op jit(solution)/shard_map/all_to_all | solution.py:132
  390.5 3.4 fusion.63
  394.0 4.3 fusion.56
  399.2 35.6 %all-reduce.1 = f32[1920]{0:T(1024)S(1)} all-reduce(f32[1920]{0:T(1024)S(1)} %pad_maximum_fusion.7), channel_id=3, replica_groups=mesh['section'=2,'dp'=16] {'dp'}, use_global_device_ids=true, to_apply=%region_17.18.clone | all-reduce | flops 1920 | bytes 15360
  434.8 3.6 all-to-all-start.3
  439.0 3.8 convolution_bitcast_fusion.2
  445.3 3.6 fusion.38
  449.0 6.1 %all-to-all-done.3 = bf16[16,128,160]{1,2,0:T(8,128)(2,1)S(1)} async-done(((bf16[16,128,160]{1,2,0:T(8,128)(2,1)}), bf16[16,128,160]{1,2,0:T(8,128)(2,1)S(1)}, u32[]{:S(2)}, u32[]{:S(2)}) %all-to-all-start.3) | async-done | bytes 655392 | tf_op jit(solution)/shard_map/all_to_all | solution.py:132
  455.1 3.5 convolution_bitcast_fusion.1
  460.0 35.8 %all-gather.20.cloned.1.call-done = bf16[2048,960]{0,1:T(8,128)(2,1)} async-done(((bf16[128,960]{0,1:T(8,128)(2,1)}), bf16[2048,960]{0,1:T(8,128)(2,1)}) %all-gather.20.cloned.1.call-update) | async-done | bytes 3932176 | tf_op jit(solution)/shard_map/all_gather | solution.py:141
  495.8 4.5 fusion.3
  (205 shorter events, 50.9 us)
Async XLA Ops:
  7.2 5.3 %copy-start.39 = (u32[32]{0:T(128)S(1)}, u32[32]{0:T(128)}, u32[]{:S(2)}) copy-start(u32[32]{0:T(128)} %constant.77) | copy-start | bytes 388
  7.2 6.5 %copy-start.42 = (bf16[1,120]{1,0:T(2,128)(2,1)S(1)}, bf16[1,120]{1,0:T(2,128)(2,1)}, u32[]{:S(2)}) copy-start(bf16[1,120]{1,0:T(2,128)(2,1)} %param.9) | copy-start | bytes 724
  7.2 42.5 %copy-start.41 = (s32[2,64]{1,0:T(2,128)S(1)}, s32[2,64]{1,0:T(2,128)}, u32[]{:S(2)}) copy-start(s32[2,64]{1,0:T(2,128)} %param.6) | copy-start | bytes 1540
  7.2 61.7 %all-gather.10.cloned.1.call-start = ((), (), s32[]{:S(2)}) async-start(), calls=%async_computation.4 | async-start | bytes 5570560 | tf_op jit(solution)/shard_map/all_gather | solution.py:141
  7.9 118.1 %all-gather.12.cloned.1.call-start = ((), (), s32[]{:S(2)}) async-start(), calls=%async_computation.5 | async-start | bytes 5570560 | tf_op jit(solution)/shard_map/all_gather | solution.py:141
  10.2 173.1 %all-gather.16.cloned.1.call-start = ((), (), s32[]{:S(2)}) async-start(), calls=%async_computation.7 | async-start | bytes 5570560 | tf_op jit(solution)/shard_map/all_gather | solution.py:141
  10.9 228.9 %all-gather.14.cloned.1.call-start = ((), (), s32[]{:S(2)}) async-start(), calls=%async_computation.6 | async-start | bytes 5570560 | tf_op jit(solution)/shard_map/all_gather | solution.py:141
  11.5 427.6 %all-gather.22.cloned.1.call-start = ((), (), s32[]{:S(2)}) async-start(), calls=%async_computation.10 | async-start | bytes 4177920 | tf_op jit(solution)/shard_map/all_gather | solution.py:141
  72.4 53.7 %copy-start.18 = (f32[1,960]{1,0:T(1,128)S(1)}, f32[1,960]{1,0:T(1,128)}, u32[]{:S(2)}) copy-start(f32[1,960]{1,0:T(1,128)} %get-tuple-element.28) | copy-start | bytes 11524
  130.7 126.2 %copy-start.27 = (f32[1,960]{1,0:T(1,128)S(1)}, f32[1,960]{1,0:T(1,128)}, u32[]{:S(2)}) copy-start(f32[1,960]{1,0:T(1,128)} %copy-done.26) | copy-start | bytes 11524
  247.2 9.0 %collective-permute-start = (bf16[128,960]{0,1:T(8,128)(2,1)S(1)}, bf16[128,960]{0,1:T(8,128)(2,1)S(1)}, u32[]{:S(2)}, u32[]{:S(2)}) collective-permute-start(bf16[128,960]{0,1:T(8,128)(2,1)S(1)} %fusion.18), channel_id=1, source_target_pairs={{0,16},{1,17},{2,18},{3,19},{4,20},{5,21},{6,22},{7,23},{8,24},{9,... | collective-permute-start | bytes 737288 | tf_op jit(solution)/shard_map/ppermute | solution.py:154
  260.5 27.1 %copy-start.4 = (bf16[15,128,64]{1,2,0:T(8,128)(2,1)}, bf16[15,128,64]{1,2,0:T(8,128)(2,1)S(1)}, u32[]{:S(2)}) copy-start(bf16[15,128,64]{1,2,0:T(8,128)(2,1)S(1)} %fusion.68) | copy-start | bytes 737284
  265.1 6.2 %copy-start.29 = (f32[128]{0:T(128)}, f32[128]{0:T(128)S(1)}, u32[]{:S(2)}) copy-start(f32[128]{0:T(128)S(1)} %get-tuple-element.38) | copy-start | bytes 1540
  266.1 179.3 %all-gather.18.cloned.1.call-start = ((), (), s32[]{:S(2)}) async-start(), calls=%async_computation.8 | async-start | bytes 4177920 | tf_op jit(solution)/shard_map/all_gather | solution.py:141
  266.6 188.4 %all-gather.24.cloned.1.call-start = ((), (), s32[]{:S(2)}) async-start(), calls=%async_computation.11 | async-start | bytes 4177920 | tf_op jit(solution)/shard_map/all_gather | solution.py:141
  266.9 14.0 %slice-start = ((s8[5242880]{0:T(1024)(128)(4,1)}), s8[4194304]{0:T(1024)(128)(4,1)S(1)}, s32[]{:S(2)}) async-start(s8[5242880]{0:T(1024)(128)(4,1)} %bitcast.215), calls=%async_computation.12 | async-start | bytes 8388608
  271.4 9.5 %slice-start.1 = ((s8[5242880]{0:T(1024)(128)(4,1)}), s8[1048576]{0:T(1024)(128)(4,1)S(1)}, s32[]{:S(2)}) async-start(s8[5242880]{0:T(1024)(128)(4,1)} %bitcast.215), calls=%async_computation.13 | async-start | bytes 2097152
  276.0 7.3 %copy-start.10 = (f32[128,2560]{1,0:T(8,128)}, f32[128,2560]{1,0:T(8,128)S(1)}, u32[]{:S(2)}) copy-start(f32[128,2560]{1,0:T(8,128)S(1)} %fusion.109) | copy-start | bytes 3932164
  276.0 7.3 %slice-start.7 = ((s8[5242880]{0:T(1024)(128)(4,1)}), s8[4194304]{0:T(1024)(128)(4,1)S(1)}, s32[]{:S(2)}) async-start(s8[5242880]{0:T(1024)(128)(4,1)} %bitcast.222), calls=%async_computation.19 | async-start | bytes 8388608
  276.0 9.3 %slice-start.4 = ((s8[5242880]{0:T(1024)(128)(4,1)}), s8[4194304]{0:T(1024)(128)(4,1)S(1)}, s32[]{:S(2)}) async-start(s8[5242880]{0:T(1024)(128)(4,1)} %bitcast.219), calls=%async_computation.16 | async-start | bytes 8388608
  290.5 9.3 %collective-permute-start.1 = (bf16[128,960]{0,1:T(8,128)(2,1)S(1)}, bf16[128,960]{0,1:T(8,128)(2,1)S(1)}, u32[]{:S(2)}, u32[]{:S(2)}) collective-permute-start(bf16[128,960]{0,1:T(8,128)(2,1)S(1)} %fusion.52), channel_id=1, source_target_pairs={{16,0},{17,1},{18,2},{19,3},{20,4},{21,5},{22,6},{23,7},{24,8},{25... | collective-permute-start | bytes 737288 | tf_op jit(solution)/shard_map/ppermute | solution.py:162
  300.5 195.3 %all-gather.20.cloned.1.call-start = ((), (), s32[]{:S(2)}) async-start(), calls=%async_computation.9 | async-start | bytes 4177920 | tf_op jit(solution)/shard_map/all_gather | solution.py:141
  307.1 5.2 %copy-start.7 = (bf16[128,2560]{1,0:T(8,128)(2,1)}, bf16[128,2560]{1,0:T(8,128)(2,1)S(1)}, u32[]{:S(2)}) copy-start(bf16[128,2560]{1,0:T(8,128)(2,1)S(1)} %get-tuple-element.15) | copy-start | bytes 1966084
  307.1 9.6 %copy-start.8 = (bf16[128,2560]{1,0:T(8,128)(2,1)}, bf16[128,2560]{1,0:T(8,128)(2,1)S(1)}, u32[]{:S(2)}) copy-start(bf16[128,2560]{1,0:T(8,128)(2,1)S(1)} %get-tuple-element.14) | copy-start | bytes 1966084
  307.1 5.2 %copy-start.19 = (f32[1,960]{1,0:T(1,128)S(1)}, f32[1,960]{1,0:T(1,128)}, u32[]{:S(2)}) copy-start(f32[1,960]{1,0:T(1,128)} %get-tuple-element.28) | copy-start | bytes 11524
  307.1 5.2 %copy-start.31 = (f32[128]{0:T(128)S(1)}, f32[128]{0:T(128)}, u32[]{:S(2)}) copy-start(f32[128]{0:T(128)} %copy-done.29) | copy-start | bytes 1540
  323.5 66.0 %copy-start.6 = (bf16[128,2560]{1,0:T(8,128)(2,1)S(1)}, bf16[128,2560]{1,0:T(8,128)(2,1)}, u32[]{:S(2)}) copy-start(bf16[128,2560]{1,0:T(8,128)(2,1)} %get-tuple-element.16) | copy-start | bytes 1966084
  323.5 26.2 %all-to-all-start = ((bf16[16,128,160]{1,2,0:T(8,128)(2,1)}), bf16[16,128,160]{1,2,0:T(8,128)(2,1)}, u32[]{:S(2)}, u32[]{:S(2)}) async-start(bf16[16,128,160]{1,2,0:T(8,128)(2,1)} %bitcast.232), calls=%async_computation | async-start | bytes 1310720 | tf_op jit(solution)/shard_map/all_to_all | solution.py:132
  327.9 62.7 %copy-start.34 = (f32[128]{0:T(128)S(1)}, f32[128]{0:T(128)}, u32[]{:S(2)}) copy-start(f32[128]{0:T(128)} %copy-done.32) | copy-start | bytes 1540
  349.6 29.6 %all-to-all-start.2 = ((bf16[16,128,160]{1,2,0:T(8,128)(2,1)}), bf16[16,128,160]{1,2,0:T(8,128)(2,1)}, u32[]{:S(2)}, u32[]{:S(2)}) async-start(bf16[16,128,160]{1,2,0:T(8,128)(2,1)} %bitcast.231), calls=%async_computation.2 | async-start | bytes 1310720 | tf_op jit(solution)/shard_map/all_to_all | solution.py:132
  379.2 55.6 %all-to-all-start.1 = ((bf16[16,128,160]{1,2,0:T(8,128)(2,1)}), bf16[16,128,160]{1,2,0:T(8,128)(2,1)}, u32[]{:S(2)}, u32[]{:S(2)}) async-start(bf16[16,128,160]{1,2,0:T(8,128)(2,1)} %bitcast.230), calls=%async_computation.1 | async-start | bytes 1310720 | tf_op jit(solution)/shard_map/all_to_all | solution.py:132
  434.8 20.2 %all-to-all-start.3 = ((bf16[16,128,160]{1,2,0:T(8,128)(2,1)}), bf16[16,128,160]{1,2,0:T(8,128)(2,1)S(1)}, u32[]{:S(2)}, u32[]{:S(2)}) async-start(bf16[16,128,160]{1,2,0:T(8,128)(2,1)} %bitcast.229), calls=%async_computation.3 | async-start | bytes 1310720 | tf_op jit(solution)/shard_map/all_to_all | solution.py:132
  (34 other events, 85.0 us)
Sparse Core Ops, SparseCore 0:
  10.3 58.5 all-gather.9
  71.7 54.2 all-gather.11
  128.9 54.3 all-gather.15
  185.4 54.3 all-gather.13
  266.2 50.6 all-gather.21
  318.9 68.8 all-gather.17
  389.9 53.6 all-gather.23
  445.8 49.9 all-gather.19
